TPU v7x, 32 devices: a whole 2x2x4 slice. The times are simulated.
32 devices in a mesh: groups: 2 (over x), dom: 16 (over z, y, core).
Axes of the slice: x: 2, y: 2, z: 4, core: 2. Of those that a mesh axis runs over, the one named last changes fastest.
Arguments:
- source: bfloat16 [72, 262144], P(None, ('groups', 'dom')), parts along dimension 1, may hold values from -6 to 6
- tile_weight: bfloat16 [8192, 128, 128], P('dom'), may hold values from -0.0625 to 0.0625
- tile_source: int32 [8192], P('dom'), may hold values from 0 to 127
- tile_slot: int32 [8192], P('dom'), may hold values from 0 to 15
- tile_count: int32 [16], P('dom'), may hold values from 64 to 512, as said below
- dest_block: int32 [256], P('dom'), may hold values from 0 to 63, as said below
- embed_weight: bfloat16 [1152, 1024], replicated, may hold values from -0.1875 to 0.1875
- embed_bias: float32 [1024], replicated, may hold values from -3 to 3
Outputs:
- remapped: bfloat16 [128, 72, 128], P(('groups', 'dom')), parts along dimension 0
- embedded: bfloat16 [1024, 1024], P(('groups', 'dom')), parts along dimension 0
There are 2 independent parts, one for each index of `groups`. A program takes and returns all parts, laid end to end along the dimension named above; an argument that names none is the same for every part. Nothing has to cross between parts.
Inputs may be any that keep to these rules, and one draw needn't show every extreme that they name: `tile_count`: number of live tiles of each device; the later tile slots are unused. Some device has all 512 tiles live. `dest_block`: the owner of target block b is device b // 4. Within one device's 16 entries the blocks are distinct and at most 2 of them belong to any one owner; on every device some owner has exactly 2.
All inputs are finite; a program needn't handle non-finite values.
Results may differ from a plain program's by a relative error of at most 0.0046.
Values may be sent and summed in bfloat16 or wider, within the bound.
A program may use at most 128 MiB of HBM per device.

v0:
```python
import functools

import jax
import jax.numpy as jnp
from jax import lax
from jax.experimental import pallas as pl
from jax.experimental.pallas import tpu as pltpu
from jax.sharding import PartitionSpec as P

PATCH = 4
CAP = 2
TB_DEV = 4
QUAD = 4
UNROLL = 4


def first_tiles(total):
    return total * 3 // 8


def rims_kernel(source_ref, slow_ref, fast_ref, sems):
    odd = lax.rem(lax.axis_index("dom"), 2)
    rim = slow_ref.shape[1]
    rest = source_ref.shape[1] - rim
    copies = [
        pltpu.make_async_copy(
            source_ref.at[:, pl.ds(pl.multiple_of(start, 128), rim)], target, sems.at[i]
        )
        for i, (start, target) in enumerate(
            ((odd * rest, slow_ref), ((1 - odd) * rest, fast_ref))
        )
    ]
    for copy in copies:
        copy.start()
    for copy in copies:
        copy.wait()


def tiles_kernel(
    order_ref,
    count_ref,
    weight_ref,
    own_ref,
    fast_ref,
    slow_ref,
    out_ref,
    cells,
    weights,
    acc,
    sems,
):
    first = first_tiles(weight_ref.shape[0])
    copies = [
        pltpu.make_async_copy(weight_ref.at[part], weights.at[part], sems.at[i])
        for i, part in enumerate((pl.ds(0, first), pl.ds(first, weight_ref.shape[0] - first)))
    ]
    for copy in copies:
        copy.start()
    own_blocks = own_ref.shape[1] // 128
    rim_blocks = fast_ref.shape[1] // 128

    def fill(ref, first, blocks):
        def step(i, _):
            for j in range(4):
                b = i * 4 + j
                cells[first + b] = ref[:, pl.ds(pl.multiple_of(b * 128, 128), 128)]
            return 0

        lax.fori_loop(0, blocks // 4, step, 0)

    fill(own_ref, 0, own_blocks)
    fill(fast_ref, own_blocks, rim_blocks)
    fill(slow_ref, own_blocks + rim_blocks, rim_blocks)
    cells[own_blocks + 2 * rim_blocks] = jnp.zeros(cells.shape[1:], cells.dtype)
    acc[...] = jnp.zeros_like(acc)

    def step(group, _):
        rows, products = [], []
        for u in range(UNROLL):
            xs, ws = [], []
            for i in range(QUAD):
                code = order_ref[(group * UNROLL + u) * QUAD + i]
                if i == 0:
                    rows.append(code >> 20)
                xs.append(cells[(code >> 12) & 0xFF])
                ws.append(weights[code & 0xFFF])
            products.append(
                jnp.dot(
                    jnp.concatenate(xs, axis=1),
                    jnp.concatenate(ws, axis=0),
                    preferred_element_type=jnp.float32,
                )
            )
        for row, product in zip(rows, products):
            acc[row] += product
        return 0

    copies[0].wait()
    lax.fori_loop(0, count_ref[0], step, 0)
    copies[1].wait()
    lax.fori_loop(count_ref[0], count_ref[1], step, 0)
    peers = out_ref.shape[0]

    def store(p, _):
        for r in range(CAP):
            out_ref[p, r] = acc[p * CAP + r].astype(jnp.bfloat16)
        return 0

    lax.fori_loop(0, peers, store, 0)


def exchange_kernel(
    peers,
    out_ref,
    label_ref,
    embed_ref,
    bias_ref,
    remapped_ref,
    embedded_ref,
    incoming,
    labels,
    embed,
    padded,
    turned,
    send_sem,
    recv_sem,
    label_send_sem,
    label_recv_sem,
    embed_sem,
):
    me = lax.axis_index("dom")
    channels = out_ref.shape[2]
    barrier = pltpu.get_barrier_semaphore()

    def greet(k, _):
        pl.semaphore_signal(
            barrier,
            inc=1,
            device_id={"dom": lax.rem(me + k, peers)},
            device_id_type=pl.DeviceIdType.MESH,
        )
        return 0

    lax.fori_loop(1, peers, greet, 0)
    embed_copy = pltpu.make_async_copy(embed_ref, embed, embed_sem)
    embed_copy.start()
    pl.semaphore_wait(barrier, peers - 1)

    def copies(k):
        peer = lax.rem(me + k, peers)
        return (
            pltpu.make_async_remote_copy(
                src_ref=label_ref.at[peer],
                dst_ref=labels.at[me],
                send_sem=label_send_sem.at[k],
                recv_sem=label_recv_sem.at[k],
                device_id={"dom": peer},
                device_id_type=pl.DeviceIdType.MESH,
            ),
            pltpu.make_async_remote_copy(
                src_ref=out_ref.at[peer],
                dst_ref=incoming.at[me],
                send_sem=send_sem.at[k],
                recv_sem=recv_sem.at[k],
                device_id={"dom": peer},
                device_id_type=pl.DeviceIdType.MESH,
            ),
        )

    def send(k, _):
        for copy in copies(k):
            copy.start()
        return 0

    lax.fori_loop(1, peers, send, 0)

    def add(totals, rows, names):
        totals = list(totals)
        for r in range(CAP):
            row = rows[r].astype(jnp.float32)
            name = jnp.broadcast_to(names[r : r + 1, :], row.shape)
            for b in range(TB_DEV):
                totals[b] = totals[b] + jnp.where(name == float(b), row, 0.0)
        return tuple(totals)

    zero = jnp.zeros((channels, 128), jnp.float32)
    totals = add((zero,) * TB_DEV, out_ref[me], label_ref[me])

    def receive(k, totals):
        for copy in copies(k):
            copy.wait_recv()
        source = lax.rem(me - k + peers, peers)
        return add(totals, incoming[source], labels[source])

    totals = lax.fori_loop(1, peers, receive, totals)
    padded[...] = jnp.zeros_like(padded)
    for b in range(TB_DEV):
        rounded = totals[b].astype(jnp.bfloat16)
        remapped_ref[b] = rounded
        padded[b, pl.ds(0, channels), :] = rounded.astype(jnp.float32)
    for b in range(TB_DEV):
        turned[pl.ds(b * 128, 128), :] = padded[b].T
    embed_copy.wait()
    per_block = 128 // (PATCH * PATCH)
    stride = PATCH * per_block
    result = jnp.zeros(embedded_ref.shape, jnp.float32)
    for r in range(PATCH):
        for q in range(PATCH):
            parts = [
                turned[pl.ds(b * 128 + r * stride + q, per_block, stride=PATCH), :]
                for b in range(TB_DEV)
            ]
            patch = jnp.concatenate(parts, axis=0).astype(jnp.bfloat16)[:, :channels]
            result = result + jnp.dot(
                patch, embed[r * PATCH + q], preferred_element_type=jnp.float32
            )
    embedded_ref[...] = (result + bias_ref[...]).astype(jnp.bfloat16)

    def finish(k, _):
        for copy in copies(k):
            copy.wait_send()
        return 0

    lax.fori_loop(1, peers, finish, 0)


def local(
    peers,
    source,
    tile_weight,
    tile_source,
    tile_slot,
    tile_count,
    dest_block,
    embed_weight,
    embed_bias,
):
    channels, own_cells = source.shape
    block_size = tile_weight.shape[1]
    own_blocks = own_cells // block_size
    rim_blocks = own_blocks // 2
    rim = rim_blocks * block_size
    ext_blocks = own_blocks + 2 * rim_blocks
    tile_total = tile_weight.shape[0]
    slot_total = dest_block.shape[0]
    emb = embed_weight.shape[1]
    rows_out = peers * CAP
    me = lax.axis_index("dom")
    odd = me % 2
    rim_shape = jax.ShapeDtypeStruct((channels, rim), source.dtype)
    slow_part, fast_part = pl.pallas_call(
        rims_kernel,
        out_shape=(rim_shape, rim_shape),
        in_specs=[pl.BlockSpec(memory_space=pl.ANY)],
        out_specs=(pl.BlockSpec(memory_space=pl.ANY),) * 2,
        scratch_shapes=[pltpu.SemaphoreType.DMA((2,))],
        compiler_params=pltpu.CompilerParams(vmem_limit_bytes=60 * 2**20),
        name="rims",
    )(source)
    slow_pairs = [(i, (i + 1) % peers if i % 2 else (i - 1) % peers) for i in range(peers)]
    fast_pairs = [(i, i + 1 - 2 * (i % 2)) for i in range(peers)]
    fast = lax.ppermute(fast_part, "dom", fast_pairs)
    slow = lax.ppermute(slow_part, "dom", slow_pairs)

    slot_ids = jnp.arange(slot_total, dtype=jnp.int32)
    owners = dest_block // TB_DEV
    earlier = (owners[None, :] == owners[:, None]) & (slot_ids[None, :] < slot_ids[:, None])
    position = owners * CAP + jnp.sum(earlier.astype(jnp.int32), axis=1)
    out_rows = jnp.arange(rows_out, dtype=jnp.int32)
    named = jnp.sum(
        jnp.where(position[None, :] == out_rows[:, None], dest_block[None, :] % TB_DEV + 1, 0), axis=1
    ) - 1
    names = jnp.broadcast_to(
        jnp.pad(named.reshape(peers, CAP), ((0, 0), (0, 8 - CAP)))[:, :, None], (peers, 8, 128)
    ).astype(jnp.float32)

    tile_ids = jnp.arange(tile_total, dtype=jnp.int32)
    live = tile_ids < tile_count[0]
    late = (tile_ids >= first_tiles(tile_total)).astype(jnp.int32)
    key = jnp.where(live, tile_slot + late * slot_total, 2 * slot_total)
    key_ids = jnp.arange(2 * slot_total, dtype=jnp.int32)
    rank = jnp.sum(
        ((key[None, :] == key[:, None]) & (tile_ids[None, :] < tile_ids[:, None])).astype(jnp.int32),
        axis=1,
    )
    held = jnp.sum((key[None, :] == key_ids[:, None]).astype(jnp.int32), axis=1)
    quads = (held + QUAD - 1) // QUAD
    early_steps = (
        jnp.sum(jnp.where(key_ids < slot_total, quads, 0)) + UNROLL - 1
    ) // UNROLL
    before = (key_ids[None, :] < key_ids[:, None]) & (
        (key_ids[None, :] >= slot_total) | (key_ids[:, None] < slot_total)
    )
    base = jnp.sum(jnp.where(before, quads[None, :], 0), axis=1)
    base = (base + jnp.where(key_ids >= slot_total, early_steps * UNROLL, 0)) * QUAD
    unit = QUAD * UNROLL
    list_total = -(-(tile_total + (QUAD - 1) * 2 * slot_total) // unit) * unit + unit
    table = base + (jnp.concatenate([position, position]) << 12)
    entry = jnp.sum(jnp.where(key[:, None] == key_ids[None, :], table[None, :], 0), axis=1)
    place = jnp.where(live, (entry & 0xFFF) + rank, -1)
    block = jnp.where(
        tile_source < rim_blocks,
        tile_source + own_blocks + jnp.where(odd == 1, 0, rim_blocks),
        tile_source
        - rim_blocks
        + jnp.where((tile_source >= rim_blocks + own_blocks) & (odd == 1), rim_blocks, 0),
    )
    code = tile_ids | (block << 12) | ((entry >> 12) << 20)
    pad_code = (rows_out << 20) | (ext_blocks << 12)
    spots = jnp.arange(list_total, dtype=jnp.int32)
    order = (
        jnp.sum(jnp.where(place[None, :] == spots[:, None], code[None, :] - pad_code, 0), axis=1)
        + pad_code
    )
    late_steps = (
        jnp.sum(jnp.where(key_ids >= slot_total, quads, 0)) + UNROLL - 1
    ) // UNROLL
    steps = jnp.stack([early_steps, early_steps + late_steps])

    smem = pl.BlockSpec(memory_space=pltpu.SMEM)
    vmem = pl.BlockSpec(memory_space=pltpu.VMEM)
    hbm = pl.BlockSpec(memory_space=pl.ANY)
    outgoing = pl.pallas_call(
        tiles_kernel,
        out_shape=jax.ShapeDtypeStruct((peers, CAP, channels, block_size), jnp.bfloat16),
        in_specs=[smem, smem, hbm, vmem, vmem, vmem],
        out_specs=vmem,
        scratch_shapes=[
            pltpu.VMEM((ext_blocks + 1, channels, block_size), source.dtype),
            pltpu.VMEM(tile_weight.shape, tile_weight.dtype),
            pltpu.VMEM((rows_out + 1, channels, block_size), jnp.float32),
            pltpu.SemaphoreType.DMA((2,)),
        ],
        compiler_params=pltpu.CompilerParams(vmem_limit_bytes=48 * 2**20),
        cost_estimate=pl.CostEstimate(
            flops=2 * tile_total * channels * block_size**2,
            bytes_accessed=tile_weight.size * 2,
            transcendentals=0,
        ),
        name="tiles",
    )(order, steps, tile_weight, source, fast, slow)

    per_patch = PATCH * PATCH
    embed_turned = embed_weight.reshape(channels, per_patch, emb).transpose(1, 0, 2)
    patch_rows = TB_DEV * (block_size // per_patch)
    remapped, embedded = pl.pallas_call(
        functools.partial(exchange_kernel, peers),
        out_shape=(
            jax.ShapeDtypeStruct((TB_DEV, channels, block_size), jnp.bfloat16),
            jax.ShapeDtypeStruct((patch_rows, emb), jnp.bfloat16),
        ),
        in_specs=[vmem, vmem, hbm, vmem],
        out_specs=(vmem, vmem),
        scratch_shapes=[
            pltpu.VMEM((peers, CAP, channels, block_size), jnp.bfloat16),
            pltpu.VMEM((peers, 8, 128), jnp.float32),
            pltpu.VMEM((per_patch, channels, emb), jnp.bfloat16),
            pltpu.VMEM((TB_DEV, 128, 128), jnp.float32),
            pltpu.VMEM((TB_DEV * 128, 128), jnp.float32),
            pltpu.SemaphoreType.DMA((peers,)),
            pltpu.SemaphoreType.DMA((peers,)),
            pltpu.SemaphoreType.DMA((peers,)),
            pltpu.SemaphoreType.DMA((peers,)),
            pltpu.SemaphoreType.DMA,
        ],
        compiler_params=pltpu.CompilerParams(
            collective_id=0, has_side_effects=True, vmem_limit_bytes=32 * 2**20
        ),
        name="exchange",
    )(
        outgoing,
        names,
        embed_turned,
        embed_bias.reshape(1, emb),
    )
    return remapped, embedded


def solution(mesh):
    placed = (
        P(None, ("groups", "dom")),
        P("dom", None, None),
        P("dom"),
        P("dom"),
        P("dom"),
        P("dom"),
        P(),
        P(),
    )
    return jax.shard_map(
        functools.partial(local, mesh.shape["dom"]),
        mesh=mesh,
        in_specs=placed,
        out_specs=(P(("groups", "dom"), None, None), P(("groups", "dom"), None)),
        check_vma=False,
    )
```

profile of v0, /device:TPU:15, one launch (start us, length us, event | category | flops | bytes accessed | tf_op | source)
XLA Modules:
  0.0 88.7 jit_solution(11787106291352243176)
XLA Ops:
  0.6 36.9 %rims.1 = (bf16[72,4096]{1,0:T(8,128)(2,1)}, bf16[72,4096]{1,0:T(8,128)(2,1)}) custom-call(bf16[72,8192]{1,0:T(8,128)(2,1)} %own_ref.1), custom_call_target="tpu_custom_call" | custom-call | tf_op jit(solution)/shard_map/rims/pallas_call | solution.py:251
  37.5 0.7 collective-permute-start
  38.2 1.2 %collective-permute-start.1 = (bf16[72,4096]{1,0:T(8,128)(2,1)}, bf16[72,4096]{1,0:T(8,128)(2,1)}, u32[]{:S(2)}, u32[]{:S(2)}) collective-permute-start(bf16[72,4096]{1,0:T(8,128)(2,1)} %get-tuple-element.5), channel_id=1, source_target_pairs={{0,15},{1,2},{2,1},{3,4},{4,3},{5,6},{6,5},{7,8},{8,7},{9,10},{10,... | collective-permute-start | bytes 1769480 | tf_op jit(solution)/shard_map/ppermute | solution.py:263
  40.1 0.7 add_select_fusion.1
  40.8 0.1 convert_reduce_fusion.1
  40.9 0.6 select_reduce_fusion.4
  42.8 0.2 convert_reduce_fusion
  43.0 0.7 fusion.3
  43.7 0.2 convert_reduce_fusion.2
  43.9 0.1 select_reduce_fusion.3
  44.0 0.2 select_reduce_fusion.2
  44.2 0.1 fusion.4
  44.3 0.1 select_reduce_fusion.1
  44.4 0.1 sub.51
  44.5 0.0 copy-start
  44.5 3.1 %copy.13 = bf16[72,16,1024]{2,0,1:T(8,128)(2,1)S(1)} copy(bf16[72,16,1024]{2,1,0:T(8,128)(2,1)} %bitcast.12) | data formatting | bytes 4718592 | tf_op jit(solution)/shard_map/reshape | solution.py:344
  47.6 0.1 pad_add_fusion.count_ref
  47.7 0.7 add_select_fusion
  48.4 0.2 select_reduce_fusion
  48.6 0.0 copy-start.1
  48.6 0.0 collective-permute-done.fast_ref
  48.6 0.3 collective-permute-done.1.slow_ref
  48.9 0.0 copy-done
  48.9 13.1 %tiles.1.out_ref = bf16[16,2,72,128]{3,2,1,0:T(8,128)(2,1)S(1)} custom-call(s32[624]{0:T(1024)S(1)} %broadcast_add_fusion.order_ref, s32[2]{0:T(128)S(1)} %pad_add_fusion.count_ref, bf16[512,128,128]{2,1,0:T(8,128)(2,1)} %weight_ref.1, bf16[72,8192]{1,0:T(8,128)(2,1)S(1)} %copy-done, bf16[72,4096]{1,0:T(8,128)(2,1)} %collective-permute-done.fast_ref, ...), custom_call_target="tpu_custom_call" | custom-call | flops 1207959552 | bytes 16777216 | tf_op jit(solution)/shard_map/tiles/pallas_call | solution.py:323
  62.0 0.1 broadcast_in_dim.109.label_ref
  62.1 0.0 copy-done.1
  62.1 25.4 %exchange.1 = (bf16[4,72,128]{2,1,0:T(8,128)(2,1)S(1)}, bf16[32,1024]{1,0:T(8,128)(2,1)S(1)}) custom-call(bf16[16,2,72,128]{3,2,1,0:T(8,128)(2,1)S(1)} %tiles.1.out_ref, f32[16,8,128]{2,1,0:T(8,128)S(1)} %broadcast_in_dim.109.label_ref, bf16[16,72,1024]{2,1,0:T(8,128)(2,1)S(1)} %bitcast.10, f32[1,1024]{1,0:T(1,128)S(1)} %bitcast.11), custom_call_target="tpu_custom_call" | custom-call | tf_op jit(solution)/shard_map/exchange/pallas_call | solution.py:346
  87.5 0.6 copy.17
  88.1 0.6 copy.18
  (5 shorter events, 0.0 us)
Async XLA Ops:
  37.5 11.1 %collective-permute-start = (bf16[72,4096]{1,0:T(8,128)(2,1)}, bf16[72,4096]{1,0:T(8,128)(2,1)}, u32[]{:S(2)}, u32[]{:S(2)}) collective-permute-start(bf16[72,4096]{1,0:T(8,128)(2,1)} %get-tuple-element.4), channel_id=1, source_target_pairs={{0,1},{1,0},{2,3},{3,2},{4,5},{5,4},{6,7},{7,6},{8,9},{9,8},{10,11... | collective-permute-start | bytes 1769480 | tf_op jit(solution)/shard_map/ppermute | solution.py:262
  38.2 10.6 %collective-permute-start.1 = (bf16[72,4096]{1,0:T(8,128)(2,1)}, bf16[72,4096]{1,0:T(8,128)(2,1)}, u32[]{:S(2)}, u32[]{:S(2)}) collective-permute-start(bf16[72,4096]{1,0:T(8,128)(2,1)} %get-tuple-element.5), channel_id=1, source_target_pairs={{0,15},{1,2},{2,1},{3,4},{4,3},{5,6},{6,5},{7,8},{8,7},{9,10},{10,... | collective-permute-start | bytes 1769480 | tf_op jit(solution)/shard_map/ppermute | solution.py:263
  44.5 4.4 %copy-start = (bf16[72,8192]{1,0:T(8,128)(2,1)S(1)}, bf16[72,8192]{1,0:T(8,128)(2,1)}, u32[]{:S(2)}) copy-start(bf16[72,8192]{1,0:T(8,128)(2,1)} %own_ref.1) | copy-start | bytes 3538948
  48.6 13.5 %copy-start.1 = (f32[1024]{0:T(1024)S(1)}, f32[1024]{0:T(1024)}, u32[]{:S(2)}) copy-start(f32[1024]{0:T(1024)} %param.15) | copy-start | bytes 12292
where the time goes:
time: 88.5 us; the launch traced here: 88.7 us
  Pallas kernels  75.4 us (85%)
  local copies, waits for them, and re-layouts  4.49 us (5%)
  other arithmetic  4.02 us (5%)
  between operations  2.65 us (3%)
  starting transfers between devices  1.94 us (2%)
    pallas_call x1, Pallas kernels, local(): pl.pallas_call(rims_kernel, out_shape=(rim_shape, rim_shape), in_specs=[p...  36.9 us
    pallas_call x1, Pallas kernels, local(): pl.pallas_call(functools.partial(exchange_kernel, peers), out_shape=(jax....  25.4 us
    pallas_call x1, Pallas kernels, local(): pl.pallas_call(tiles_kernel, out_shape=jax.ShapeDtypeStruct((peers, CAP,...  13.1 us
    reshape x1, local copies, waits for them, and re-layouts, local(): embed_weight.reshape(channels, per_patch, emb).transpose(1, 0, 2)  3.06 us
  transfers between devices with their start and end apart: 2, of which 1 were waited for; matrix products, arithmetic and copies ran while one was open for 8% of the time, Pallas kernels for 0%

commit v1 on v0

--- a/solution.py
+++ b/solution.py
@@ -252,7 +252,7 @@
         rims_kernel,
         out_shape=(rim_shape, rim_shape),
         in_specs=[pl.BlockSpec(memory_space=pl.ANY)],
-        out_specs=(pl.BlockSpec(memory_space=pl.ANY),) * 2,
+        out_specs=(pl.BlockSpec(memory_space=pltpu.VMEM),) * 2,
         scratch_shapes=[pltpu.SemaphoreType.DMA((2,))],
         compiler_params=pltpu.CompilerParams(vmem_limit_bytes=60 * 2**20),
         name="rims",

time: 88.5 us -> 53 us (0.60); the launches traced: 88.7 us -> 52.3 us
  Pallas kernels: 75.4 us -> 38.9 us
    pallas_call x1, Pallas kernels: 36.9 us -> 2.28 us  [local(): pl.pallas_call(rims_kernel, out_shape=(rim_shape, rim_shape), in_specs=[p...]
    pallas_call x1, Pallas kernels: 25.4 us -> 23.5 us  [local(): pl.pallas_call(functools.partial(exchange_kernel, peers), out_shape=(jax....]
  transfers between devices with their start and end apart: 2 -> 2, of which waited for: 1 -> 1; matrix products, arithmetic and copies ran while one was open for 8% -> 14% of each run, Pallas kernels for 0% -> 0%
where the time goes in v1:
time: 53 us; the launch traced here: 52.3 us
  Pallas kernels  38.9 us (73%)
  local copies, waits for them, and re-layouts  4.49 us (8%)
  other arithmetic  4.02 us (8%)
  between operations  2.65 us (5%)
  starting transfers between devices  1.94 us (4%)
    pallas_call x1, Pallas kernels, local(): pl.pallas_call(functools.partial(exchange_kernel, peers), out_shape=(jax....  23.5 us
    pallas_call x1, Pallas kernels, local(): pl.pallas_call(tiles_kernel, out_shape=jax.ShapeDtypeStruct((peers, CAP,...  13.1 us
    reshape x1, local copies, waits for them, and re-layouts, local(): embed_weight.reshape(channels, per_patch, emb).transpose(1, 0, 2)  3.06 us
    pallas_call x1, Pallas kernels, local(): pl.pallas_call(rims_kernel, out_shape=(rim_shape, rim_shape), in_specs=[p...  2.28 us
    unnamed x6, local copies, waits for them, and re-layouts  1.27 us
    ppermute x1, starting transfers between devices, local(): slow = lax.ppermute(slow_part, 'dom', slow_pairs)  1.2 us
  transfers between devices with their start and end apart: 2, of which 1 were waited for; matrix products, arithmetic and copies ran while one was open for 14% of the time, Pallas kernels for 0%

profile of v1, /device:TPU:15, one launch (start us, length us, event | category | flops | bytes accessed | tf_op | source)
XLA Modules:
  0.0 52.3 jit_solution(3395281728600991772)
XLA Ops:
  0.6 2.3 %rims.1 = (bf16[72,4096]{1,0:T(8,128)(2,1)}, bf16[72,4096]{1,0:T(8,128)(2,1)}) custom-call(bf16[72,8192]{1,0:T(8,128)(2,1)} %own_ref.1), custom_call_target="tpu_custom_call" | custom-call | tf_op jit(solution)/shard_map/rims/pallas_call | solution.py:251
  2.9 0.7 %collective-permute-start = (bf16[72,4096]{1,0:T(8,128)(2,1)}, bf16[72,4096]{1,0:T(8,128)(2,1)}, u32[]{:S(2)}, u32[]{:S(2)}) collective-permute-start(bf16[72,4096]{1,0:T(8,128)(2,1)} %get-tuple-element.4), channel_id=1, source_target_pairs={{0,1},{1,0},{2,3},{3,2},{4,5},{5,4},{6,7},{7,6},{8,9},{9,8},{10,11... | collective-permute-start | bytes 1769480 | tf_op jit(solution)/shard_map/ppermute | solution.py:262
  3.7 1.2 %collective-permute-start.1 = (bf16[72,4096]{1,0:T(8,128)(2,1)}, bf16[72,4096]{1,0:T(8,128)(2,1)}, u32[]{:S(2)}, u32[]{:S(2)}) collective-permute-start(bf16[72,4096]{1,0:T(8,128)(2,1)} %get-tuple-element.5), channel_id=1, source_target_pairs={{0,15},{1,2},{2,1},{3,4},{4,3},{5,6},{6,5},{7,8},{8,7},{9,10},{10,... | collective-permute-start | bytes 1769480 | tf_op jit(solution)/shard_map/ppermute | solution.py:263
  5.5 0.7 %add_select_fusion.1 = s32[512]{0:T(512)S(1)} fusion(s32[512]{0:T(512)} %param.11, s32[]{:T(128)} %bitcast.8), kind=kLoop, calls=%fused_computation.22 | loop fusion | flops 2560 | bytes 4100 | tf_op jit(solution)/shard_map/jit(_where)/select_n | solution.py:280
  6.2 0.1 convert_reduce_fusion.1
  6.3 0.6 %select_reduce_fusion.4 = (s32[]{:T(128)}, s32[]{:T(128)}, s32[32]{0:T(128)S(1)}) fusion(s32[32]{0:T(128)S(1)} %convert_reduce_fusion.1), kind=kLoop, calls=%fused_computation.38 | loop fusion | flops 702 | bytes 264 | tf_op jit(solution)/shard_map/reduce_sum | solution.py:316
  8.2 0.2 convert_reduce_fusion
  8.5 0.7 %fusion.3 = (s32[16]{0:T(128)S(1)}, s32[16]{0:T(128)S(1)}) fusion(s32[16]{0:T(128)} %param.13), kind=kLoop, calls=%fused_computation.34 | loop fusion | flops 320 | bytes 192 | tf_op jit(solution)/shard_map/add | solution.py:271
  9.1 0.2 convert_reduce_fusion.2
  9.3 0.1 select_reduce_fusion.3
  9.5 0.2 select_reduce_fusion.2
  9.6 0.1 fusion.4
  9.7 0.1 select_reduce_fusion.1
  9.8 0.1 sub.51
  9.9 0.0 copy-start
  9.9 3.1 %copy.13 = bf16[72,16,1024]{2,0,1:T(8,128)(2,1)S(1)} copy(bf16[72,16,1024]{2,1,0:T(8,128)(2,1)} %bitcast.12) | data formatting | bytes 4718592 | tf_op jit(solution)/shard_map/reshape | solution.py:344
  13.0 0.1 pad_add_fusion.count_ref
  13.1 0.7 %add_select_fusion = (s32[512]{0:T(512)S(1)}, s32[512]{0:T(512)S(1)}) fusion(s32[512]{0:T(512)S(1)} %convert_reduce_fusion, s32[512]{0:T(512)S(1)} %select_reduce_fusion.1, s32[]{:T(128)} %bitcast.9, pred[]{:T(512)S(6)} %eq.101, s32[512]{0:T(512)} %param.10, s32[]{:T(128)S(6)} %select_n.99), kind=kLoop, calls=%fused_computation.21 | loop fusion | flops 9728 | bytes 10249 | tf_op jit(solution)/shard_map/jit(_where)/select_n | solution.py:300
  13.8 0.2 select_reduce_fusion
  14.0 0.0 copy-start.1
  14.0 0.0 collective-permute-done.fast_ref
  14.0 0.3 collective-permute-done.1.slow_ref
  14.3 0.0 copy-done
  14.3 13.1 %tiles.1.out_ref = bf16[16,2,72,128]{3,2,1,0:T(8,128)(2,1)S(1)} custom-call(s32[624]{0:T(1024)S(1)} %broadcast_add_fusion.order_ref, s32[2]{0:T(128)S(1)} %pad_add_fusion.count_ref, bf16[512,128,128]{2,1,0:T(8,128)(2,1)} %weight_ref.1, bf16[72,8192]{1,0:T(8,128)(2,1)S(1)} %copy-done, bf16[72,4096]{1,0:T(8,128)(2,1)} %collective-permute-done.fast_ref, ...), custom_call_target="tpu_custom_call" | custom-call | flops 1207959552 | bytes 16777216 | tf_op jit(solution)/shard_map/tiles/pallas_call | solution.py:323
  27.4 0.1 broadcast_in_dim.109.label_ref
  27.5 0.0 copy-done.1
  27.5 23.5 %exchange.1 = (bf16[4,72,128]{2,1,0:T(8,128)(2,1)S(1)}, bf16[32,1024]{1,0:T(8,128)(2,1)S(1)}) custom-call(bf16[16,2,72,128]{3,2,1,0:T(8,128)(2,1)S(1)} %tiles.1.out_ref, f32[16,8,128]{2,1,0:T(8,128)S(1)} %broadcast_in_dim.109.label_ref, bf16[16,72,1024]{2,1,0:T(8,128)(2,1)S(1)} %bitcast.10, f32[1,1024]{1,0:T(1,128)S(1)} %bitcast.11), custom_call_target="tpu_custom_call" | custom-call | tf_op jit(solution)/shard_map/exchange/pallas_call | solution.py:346
  51.0 0.6 %copy.17 = bf16[4,72,128]{2,1,0:T(8,128)(2,1)} copy(bf16[4,72,128]{2,1,0:T(8,128)(2,1)S(1)} %get-tuple-element.17) | data formatting | bytes 147456
  51.7 0.6 %copy.18 = bf16[32,1024]{1,0:T(8,128)(2,1)} copy(bf16[32,1024]{1,0:T(8,128)(2,1)S(1)} %get-tuple-element.18) | data formatting | bytes 131072
  (5 shorter events, 0.0 us)
Async XLA Ops:
  2.9 11.1 %collective-permute-start = (bf16[72,4096]{1,0:T(8,128)(2,1)}, bf16[72,4096]{1,0:T(8,128)(2,1)}, u32[]{:S(2)}, u32[]{:S(2)}) collective-permute-start(bf16[72,4096]{1,0:T(8,128)(2,1)} %get-tuple-element.4), channel_id=1, source_target_pairs={{0,1},{1,0},{2,3},{3,2},{4,5},{5,4},{6,7},{7,6},{8,9},{9,8},{10,11... | collective-permute-start | bytes 1769480 | tf_op jit(solution)/shard_map/ppermute | solution.py:262
  3.7 10.6 %collective-permute-start.1 = (bf16[72,4096]{1,0:T(8,128)(2,1)}, bf16[72,4096]{1,0:T(8,128)(2,1)}, u32[]{:S(2)}, u32[]{:S(2)}) collective-permute-start(bf16[72,4096]{1,0:T(8,128)(2,1)} %get-tuple-element.5), channel_id=1, source_target_pairs={{0,15},{1,2},{2,1},{3,4},{4,3},{5,6},{6,5},{7,8},{8,7},{9,10},{10,... | collective-permute-start | bytes 1769480 | tf_op jit(solution)/shard_map/ppermute | solution.py:263
  9.9 4.4 %copy-start = (bf16[72,8192]{1,0:T(8,128)(2,1)S(1)}, bf16[72,8192]{1,0:T(8,128)(2,1)}, u32[]{:S(2)}) copy-start(bf16[72,8192]{1,0:T(8,128)(2,1)} %own_ref.1) | copy-start | bytes 3538948
  14.0 13.5 %copy-start.1 = (f32[1024]{0:T(1024)S(1)}, f32[1024]{0:T(1024)}, u32[]{:S(2)}) copy-start(f32[1024]{0:T(1024)} %param.15) | copy-start | bytes 12292
